TPU v7x, 32 devices: a whole 2x2x4 slice. The times are simulated.
32 devices in a mesh: row: 8 (over z, y), col: 4 (over x, core).
Axes of the slice: x: 2, y: 2, z: 4, core: 2. Of those that a mesh axis runs over, the one named last changes fastest.
Arguments:
- tokens: bfloat16 [8192, 1472], P(('row', 'col')), may hold values from -6 to 6
- lengths: int32 [8], P('row'), may hold values from 200 to 1024, as said below
- out_grad: bfloat16 [8192, 1472], P(('row', 'col')), may hold values from -6 to 6
- gain_attn: float32 [1472], replicated, may hold values from 0.5 to 1.5
- w_query: bfloat16 [1472, 384], P('row', 'col'), may hold values from -0.0390625 to 0.0390625
- w_key: bfloat16 [1472, 384], P('row', 'col'), may hold values from -0.15625 to 0.15625
- w_value: bfloat16 [1472, 384], P('row', 'col'), may hold values from -0.15625 to 0.15625
- w_attn_out: bfloat16 [384, 1472], P('col', 'row'), may hold values from -1.25 to 1.25
- bias_table: float32 [32, 6], replicated, may hold values from -4 to 4
- gain_ff: float32 [1472], replicated, may hold values from 0.5 to 1.5
- w_gate: bfloat16 [1472, 3584], P('row', 'col'), may hold values from -0.15625 to 0.15625
- w_up: bfloat16 [1472, 3584], P('row', 'col'), may hold values from -0.15625 to 0.15625
- w_down: bfloat16 [3584, 1472], P('col', 'row'), may hold values from -0.09375 to 0.09375
Outputs:
- output: bfloat16 [8192, 1472], P(('row', 'col'))
- input_grad: float32 [8192, 1472], P(('row', 'col'))
- grad_gain_attn: float32 [1472], replicated
- grad_query: float32 [1472, 384], P('row', 'col')
- grad_key: float32 [1472, 384], P('row', 'col')
- grad_value: float32 [1472, 384], P('row', 'col')
- grad_attn_out: float32 [384, 1472], P('col', 'row')
- grad_bias: float32 [32, 6], replicated
- grad_gain_ff: float32 [1472], replicated
- grad_gate: float32 [1472, 3584], P('row', 'col')
- grad_up: float32 [1472, 3584], P('row', 'col')
- grad_down: float32 [3584, 1472], P('col', 'row')
Inputs may be any that keep to these rules, and one draw needn't show every extreme that they name: Each sequence holds one document in its first lengths slots, the rest of its 1024 slots are padding; some sequence is full.
All inputs are finite; a program needn't handle non-finite values.
Results may differ from a plain program's by a relative error of at most 0.023.
Values may be sent and summed in bfloat16 or wider, within the bound.
No kernel may reach another device: no remote copies, remote signals or barrier semaphores. Data moves between devices by JAX's collectives and lax.ppermute only.
A program may use at most 192 MiB of HBM per device.

v0:
```python
import jax
import jax.numpy as jnp
from jax import lax
from jax.sharding import PartitionSpec as P

HEADS = 6
HEAD_DIM = 64
EPSILON = 1e-06
FAR_STEPS = (12, 16, 23, 32, 46, 64, 91)
PRECISION_MAX = lax.Precision.HIGHEST


def bucket_index(offsets):
    magnitude = jnp.abs(offsets)
    far_bucket = 8 + sum(((magnitude >= limit).astype(jnp.int32) for limit in FAR_STEPS))
    near_bucket = jnp.where(magnitude < 8, magnitude, far_bucket)
    return near_bucket + jnp.where(offsets > 0, 16, 0)


def root_scale(values, gain):
    return values * lax.rsqrt(jnp.mean(values * values, axis=-1, keepdims=True) + EPSILON) * gain


def gated_product(gate_part, up_part):
    return jax.nn.gelu(gate_part, approximate=True) * up_part


def matmul(left, right):
    return jnp.dot(left, right, preferred_element_type=jnp.float32)


def spread_rows(line, row_total, column_total):
    line_width = line.shape[0]
    tiled_line = jnp.tile(line, row_total + 1)[: row_total * (line_width + 1)]
    shifted = tiled_line.reshape(row_total, line_width + 1)
    return shifted[::-1, :column_total]


def fold_rows(matrix):
    row_total, column_total = matrix.shape
    padded = jnp.pad(matrix[::-1], ((0, 0), (0, row_total)))
    flattened = padded.reshape(-1)[: row_total * (column_total + row_total - 1)]
    return jnp.sum(flattened.reshape(row_total, column_total + row_total - 1), axis=0)


def body(
    tokens,
    lengths,
    out_grad,
    gain_attn,
    w_query,
    w_key,
    w_value,
    w_attn_out,
    bias_table,
    gain_ff,
    w_gate,
    w_up,
    w_down,
):
    tok_rows = tokens.shape[0]
    seq_len = tok_rows * lax.axis_size("col")
    first_row = lax.axis_index("col") * tok_rows
    doc_length = lengths[0]
    local_pos = first_row + jnp.arange(tok_rows, dtype=jnp.int32)
    row_mask = (local_pos < doc_length).astype(jnp.float32)[:, None]
    key_valid = jnp.arange(seq_len, dtype=jnp.int32) < doc_length
    row_query, row_key, row_value, row_out, full_gate, full_up, full_down = (
        lax.all_gather(w_query, "row", axis=0, tiled=True),
        lax.all_gather(w_key, "row", axis=0, tiled=True),
        lax.all_gather(w_value, "row", axis=0, tiled=True),
        lax.all_gather(w_attn_out, "row", axis=1, tiled=True),
        lax.all_gather(w_gate, "row", axis=0, tiled=True),
        lax.all_gather(w_up, "row", axis=0, tiled=True),
        lax.all_gather(w_down, "row", axis=1, tiled=True),
    )
    full_query, full_key, full_value, full_out = (
        lax.all_gather(row_query, "col", axis=1, tiled=True),
        lax.all_gather(row_key, "col", axis=1, tiled=True),
        lax.all_gather(row_value, "col", axis=1, tiled=True),
        lax.all_gather(row_out, "col", axis=0, tiled=True),
    )
    inputs_float = tokens.astype(jnp.float32)
    normed = root_scale(inputs_float, gain_attn).astype(jnp.bfloat16)
    queries = matmul(normed, full_query).astype(jnp.bfloat16)
    own_keys = matmul(normed, full_key).astype(jnp.bfloat16)
    own_values = matmul(normed, full_value).astype(jnp.bfloat16)
    keys_all, values_all = (
        lax.all_gather(own_keys, "col", axis=0, tiled=True),
        lax.all_gather(own_values, "col", axis=0, tiled=True),
    )
    offset_span = seq_len + tok_rows - 1
    offsets = jnp.arange(offset_span, dtype=jnp.int32) - (tok_rows - 1) - first_row
    onehot = (
        bucket_index(offsets)[:, None] == jnp.arange(bias_table.shape[0], dtype=jnp.int32)[None, :]
    ).astype(jnp.float32)
    bias_lines = jnp.dot(
        onehot, bias_table, precision=PRECISION_MAX, preferred_element_type=jnp.float32
    ).T

    def head_scores(head_index):
        head_start = head_index * HEAD_DIM
        query_head = queries[:, head_start : head_start + HEAD_DIM]
        key_head = keys_all[:, head_start : head_start + HEAD_DIM]
        scores = jnp.einsum("qd,kd->qk", query_head, key_head, preferred_element_type=jnp.float32)
        scores = scores + spread_rows(bias_lines[head_index], tok_rows, seq_len)
        return jnp.where(key_valid[None, :], scores, -1e30)

    contexts = []
    log_totals = []
    for head_index in range(HEADS):
        masked = head_scores(head_index)
        row_peak = jnp.max(masked, axis=1, keepdims=True)
        log_total = row_peak + jnp.log(jnp.sum(jnp.exp(masked - row_peak), axis=1, keepdims=True))
        attention = jnp.exp(masked - log_total)
        value_head = values_all[:, head_index * HEAD_DIM : (head_index + 1) * HEAD_DIM]
        contexts.append(
            jnp.einsum(
                "qk,kd->qd",
                attention.astype(jnp.bfloat16),
                value_head,
                preferred_element_type=jnp.float32,
            )
        )
        log_totals.append(log_total)
    context = jnp.concatenate(contexts, axis=1).astype(jnp.bfloat16)
    hidden = inputs_float + matmul(context, full_out)
    normed_ff = root_scale(hidden, gain_ff).astype(jnp.bfloat16)
    grad_out = out_grad.astype(jnp.float32) * row_mask
    ff_rows = lax.all_gather(normed_ff, "col", axis=0, tiled=True)
    hidden_ff = gated_product(matmul(ff_rows, full_gate), matmul(ff_rows, full_up)).astype(
        jnp.bfloat16
    )
    ff_branch = lax.psum_scatter(
        matmul(hidden_ff, full_down).astype(jnp.bfloat16), "col", scatter_dimension=0, tiled=True
    ).astype(jnp.float32)
    output = (row_mask * (hidden + ff_branch)).astype(jnp.bfloat16)
    cot_rows = lax.all_gather(grad_out.astype(jnp.bfloat16), "col", axis=0, tiled=True)
    gate_proj = matmul(ff_rows, full_gate)
    up_proj = matmul(ff_rows, full_up)
    product_value, gelu_pull = jax.vjp(gated_product, gate_proj, up_proj)
    hidden_back = product_value.astype(jnp.bfloat16)
    grad_down_part = jnp.einsum(
        "rf,rd->fd", hidden_back, cot_rows, preferred_element_type=jnp.float32
    )
    grad_hidden_ff = jnp.einsum(
        "rd,fd->rf", cot_rows, full_down, preferred_element_type=jnp.float32
    )
    grad_gate_float, grad_up_float = gelu_pull(grad_hidden_ff)
    grad_gate_proj = grad_gate_float.astype(jnp.bfloat16)
    grad_up_proj = grad_up_float.astype(jnp.bfloat16)
    grad_gate_part = jnp.einsum(
        "rd,rf->df", ff_rows, grad_gate_proj, preferred_element_type=jnp.float32
    )
    grad_up_part = jnp.einsum(
        "rd,rf->df", ff_rows, grad_up_proj, preferred_element_type=jnp.float32
    )
    grad_normed_ff = lax.psum_scatter(
        (
            jnp.einsum("rf,df->rd", grad_gate_proj, full_gate, preferred_element_type=jnp.float32)
            + jnp.einsum("rf,df->rd", grad_up_proj, full_up, preferred_element_type=jnp.float32)
        ).astype(jnp.bfloat16),
        "col",
        scatter_dimension=0,
        tiled=True,
    ).astype(jnp.float32)
    norm_value, norm_pull = jax.vjp(root_scale, hidden, gain_ff)
    grad_hidden_norm, grad_gain_ff_part = norm_pull(grad_normed_ff)
    grad_hidden = grad_out + grad_hidden_norm
    grad_attn = grad_hidden.astype(jnp.bfloat16)
    grad_out_part = jnp.einsum("ti,td->id", context, grad_attn, preferred_element_type=jnp.float32)
    grad_context = jnp.einsum(
        "td,id->ti", grad_attn, full_out, preferred_element_type=jnp.float32
    ).astype(jnp.bfloat16)
    grad_query_heads = []
    grad_key_heads = []
    grad_value_heads = []
    diagonal_lines = []
    for head_index in range(HEADS):
        head_start = head_index * HEAD_DIM
        query_head = queries[:, head_start : head_start + HEAD_DIM]
        key_head = keys_all[:, head_start : head_start + HEAD_DIM]
        value_head = values_all[:, head_start : head_start + HEAD_DIM]
        grad_ctx_head = grad_context[:, head_start : head_start + HEAD_DIM]
        attention = jnp.exp(head_scores(head_index) - log_totals[head_index])
        grad_attention = jnp.einsum(
            "qd,kd->qk", grad_ctx_head, value_head, preferred_element_type=jnp.float32
        )
        row_inner = jnp.sum(attention * grad_attention, axis=1, keepdims=True)
        grad_scores = (attention * (grad_attention - row_inner)).astype(jnp.bfloat16)
        grad_query_heads.append(
            jnp.einsum("qk,kd->qd", grad_scores, key_head, preferred_element_type=jnp.float32)
        )
        grad_key_heads.append(
            jnp.einsum("qk,qd->kd", grad_scores, query_head, preferred_element_type=jnp.float32)
        )
        grad_value_heads.append(
            jnp.einsum(
                "qk,qd->kd",
                attention.astype(jnp.bfloat16),
                grad_ctx_head,
                preferred_element_type=jnp.float32,
            )
        )
        diagonal_lines.append(fold_rows(grad_scores.astype(jnp.float32)))
    grad_bias_part = jnp.einsum(
        "eb,he->bh",
        onehot,
        jnp.stack(diagonal_lines, axis=0),
        precision=PRECISION_MAX,
        preferred_element_type=jnp.float32,
    )
    grad_queries = jnp.concatenate(grad_query_heads, axis=1).astype(jnp.bfloat16)
    key_partial = jnp.concatenate(grad_key_heads, axis=1)
    value_partial = jnp.concatenate(grad_value_heads, axis=1)
    key_summed, value_summed = (
        lax.psum_scatter(
            key_partial.astype(jnp.bfloat16), "col", scatter_dimension=0, tiled=True
        ).astype(jnp.float32),
        lax.psum_scatter(
            value_partial.astype(jnp.bfloat16), "col", scatter_dimension=0, tiled=True
        ).astype(jnp.float32),
    )
    grad_keys = key_summed.astype(jnp.bfloat16)
    grad_values = value_summed.astype(jnp.bfloat16)
    grad_query_part = jnp.einsum(
        "td,ti->di", normed, grad_queries, preferred_element_type=jnp.float32
    )
    grad_key_part = jnp.einsum("td,ti->di", normed, grad_keys, preferred_element_type=jnp.float32)
    grad_value_part = jnp.einsum(
        "td,ti->di", normed, grad_values, preferred_element_type=jnp.float32
    )
    grad_normed = (
        jnp.einsum("ti,di->td", grad_queries, full_query, preferred_element_type=jnp.float32)
        + jnp.einsum("ti,di->td", grad_keys, full_key, preferred_element_type=jnp.float32)
        + jnp.einsum("ti,di->td", grad_values, full_value, preferred_element_type=jnp.float32)
    )
    first_value, first_pull = jax.vjp(root_scale, inputs_float, gain_attn)
    grad_input_norm, grad_gain_attn_part = first_pull(grad_normed)
    input_grad = grad_hidden + grad_input_norm
    cols_query, cols_key, cols_value, cols_out = (
        lax.psum_scatter(
            grad_query_part.astype(jnp.bfloat16), "col", scatter_dimension=1, tiled=True
        ).astype(jnp.float32),
        lax.psum_scatter(
            grad_key_part.astype(jnp.bfloat16), "col", scatter_dimension=1, tiled=True
        ).astype(jnp.float32),
        lax.psum_scatter(
            grad_value_part.astype(jnp.bfloat16), "col", scatter_dimension=1, tiled=True
        ).astype(jnp.float32),
        lax.psum_scatter(
            grad_out_part.astype(jnp.bfloat16), "col", scatter_dimension=0, tiled=True
        ).astype(jnp.float32),
    )
    grad_query, grad_key, grad_value, grad_attn_out, grad_gate, grad_up, grad_down = (
        lax.psum_scatter(
            cols_query.astype(jnp.bfloat16), "row", scatter_dimension=0, tiled=True
        ).astype(jnp.float32),
        lax.psum_scatter(
            cols_key.astype(jnp.bfloat16), "row", scatter_dimension=0, tiled=True
        ).astype(jnp.float32),
        lax.psum_scatter(
            cols_value.astype(jnp.bfloat16), "row", scatter_dimension=0, tiled=True
        ).astype(jnp.float32),
        lax.psum_scatter(
            cols_out.astype(jnp.bfloat16), "row", scatter_dimension=1, tiled=True
        ).astype(jnp.float32),
        lax.psum_scatter(
            grad_gate_part.astype(jnp.bfloat16), "row", scatter_dimension=0, tiled=True
        ).astype(jnp.float32),
        lax.psum_scatter(
            grad_up_part.astype(jnp.bfloat16), "row", scatter_dimension=0, tiled=True
        ).astype(jnp.float32),
        lax.psum_scatter(
            grad_down_part.astype(jnp.bfloat16), "row", scatter_dimension=1, tiled=True
        ).astype(jnp.float32),
    )
    grad_gain_attn, grad_bias, grad_gain_ff = lax.psum(
        (grad_gain_attn_part, grad_bias_part, grad_gain_ff_part), ("row", "col")
    )
    return (
        output,
        input_grad,
        grad_gain_attn,
        grad_query,
        grad_key,
        grad_value,
        grad_attn_out,
        grad_bias,
        grad_gain_ff,
        grad_gate,
        grad_up,
        grad_down,
    )


def solution(mesh):
    placed = (
        P(("row", "col"), None),
        P("row"),
        P(("row", "col"), None),
        P(),
        P("row", "col"),
        P("row", "col"),
        P("row", "col"),
        P("col", "row"),
        P(),
        P(),
        P("row", "col"),
        P("row", "col"),
        P("col", "row"),
    )
    return jax.shard_map(
        body,
        mesh=mesh,
        in_specs=placed,
        out_specs=(
            P(("row", "col"), None),
            P(("row", "col"), None),
            P(),
            P("row", "col"),
            P("row", "col"),
            P("row", "col"),
            P("col", "row"),
            P(),
            P(),
            P("row", "col"),
            P("row", "col"),
            P("col", "row"),
        ),
        check_vma=False,
    )
```

profile of v0, /device:TPU:0, one launch (start us, length us, event | category | flops | bytes accessed | tf_op | source)
XLA Modules:
  0.0 1051.5 jit_solution(16021638598668254350)
XLA Ops:
  7.3 32.9 %all_gather.47 = bf16[1472,96]{1,0:T(8,128)(2,1)S(1)} all-gather(bf16[184,96]{1,0:T(8,128)(2,1)} %param.18), channel_id=1, replica_groups=mesh['row'=8,'col'=4] {'row'}, dimensions={0}, use_global_device_ids=true | all-gather | bytes 317952 | tf_op jit(solution)/shard_map/all_gather | solution.py:70
  41.2 31.2 %all_gather.45 = bf16[1472,96]{1,0:T(8,128)(2,1)S(1)} all-gather(bf16[184,96]{1,0:T(8,128)(2,1)} %param.17), channel_id=1, replica_groups=mesh['row'=8,'col'=4] {'row'}, dimensions={0}, use_global_device_ids=true | all-gather | bytes 317952 | tf_op jit(solution)/shard_map/all_gather | solution.py:69
  73.3 31.1 %all_gather.50 = bf16[1472,96]{1,0:T(8,128)(2,1)S(1)} all-gather(bf16[184,96]{1,0:T(8,128)(2,1)S(1)} %copy-done.53), channel_id=1, replica_groups=mesh['row'=8,'col'=4] {'row'}, dimensions={0}, use_global_device_ids=true | all-gather | bytes 317952 | tf_op jit(solution)/shard_map/all_gather | solution.py:71
  105.4 30.9 %all_gather.53 = bf16[96,1472]{0,1:T(8,128)(2,1)S(1)} all-gather(bf16[96,184]{0,1:T(8,128)(2,1)S(1)} %copy-done.54), channel_id=1, replica_groups=mesh['row'=8,'col'=4] {'row'}, dimensions={1}, use_global_device_ids=true | all-gather | bytes 317952 | tf_op jit(solution)/shard_map/all_gather | solution.py:72
  208.1 9.1 all_gather.49
  235.3 8.9 all_gather.52
  255.9 24.4 %all-gather.18.cloned.1.call-done = bf16[1024,1472]{0,1:T(8,128)(2,1)} async-done(((bf16[256,1472]{0,1:T(8,128)(2,1)}), bf16[1024,1472]{0,1:T(8,128)(2,1)}) %all-gather.18.cloned.1.call-update) | async-done | bytes 3014672 | tf_op jit(solution)/shard_map/all_gather | solution.py:130
  280.3 7.9 fusion.151
  288.2 49.2 %all-gather.22.cloned.1.call-done = bf16[1472,896]{1,0:T(8,128)(2,1)} async-done(((bf16[184,896]{1,0:T(8,128)(2,1)}), bf16[1472,896]{1,0:T(8,128)(2,1)}) %all-gather.22.cloned.1.call-update) | async-done | bytes 2637840 | tf_op jit(solution)/shard_map/all_gather | solution.py:74
  337.4 7.9 fusion.152
  345.3 20.4 %all-gather.26.cloned.1.call-done = bf16[1024,1472]{0,1:T(8,128)(2,1)} async-done(((bf16[256,1472]{0,1:T(8,128)(2,1)}), bf16[1024,1472]{0,1:T(8,128)(2,1)}) %all-gather.26.cloned.1.call-update) | async-done | bytes 3014672 | tf_op jit(solution)/shard_map/all_gather | solution.py:138
  365.7 57.1 %all-gather.24.cloned.1.call-done = bf16[896,1472]{0,1:T(8,128)(2,1)} async-done(((bf16[896,184]{0,1:T(8,128)(2,1)}), bf16[896,1472]{0,1:T(8,128)(2,1)}) %all-gather.24.cloned.1.call-update) | async-done | bytes 2637840 | tf_op jit(solution)/shard_map/all_gather | solution.py:75
  422.8 12.6 %multiply_convert_fusion = (bf16[1024,896]{1,0:T(8,128)(2,1)S(1)}, bf16[1024,896]{1,0:T(8,128)(2,1)S(1)}, bf16[1024,896]{1,0:T(8,128)(2,1)}) fusion(f32[1024,896]{1,0:T(8,128)} %fusion.151, f32[1024,896]{1,0:T(8,128)} %fusion.152, bf16[1024,1472]{0,1:T(8,128)(2,1)} %all-gather.26.cloned.1.call-done, bf16[896,1472]{0,1:T(8,128)(2,1)} %all-gather.24.cloned.1.call-done), kind=kOutput, calls=%fused_computation.11 | convolution fusion | flops 2724986880 | bytes 18497536 | tf_op jit(solution)/shard_map/rd,fd->rf/dot_general | solution.py:146
  450.9 28.5 %reduce-scatter.24.cloned.1.call-done = bf16[256,1472]{0,1:T(8,128)(2,1)} async-done(((bf16[1024,1472]{0,1:T(8,128)(2,1)}), bf16[256,1472]{0,1:T(8,128)(2,1)}) %reduce-scatter.24.cloned.1.call-update) | async-done | bytes 753680 | tf_op jit(solution)/shard_map/reduce_scatter | solution.py:158
  482.3 37.0 %reduce-scatter.22.cloned.1.call-done = bf16[256,1472]{0,1:T(8,128)(2,1)} async-done(((bf16[1024,1472]{0,1:T(8,128)(2,1)}), bf16[256,1472]{0,1:T(8,128)(2,1)}) %reduce-scatter.22.cloned.1.call-update) | async-done | bytes 753680 | tf_op jit(solution)/shard_map/reduce_scatter | solution.py:134
  593.7 80.1 %reduce-scatter.38.cloned.1.call-done = bf16[184,896]{1,0:T(8,128)(2,1)} async-done(((bf16[1472,896]{1,0:T(8,128)(2,1)}), bf16[184,896]{1,0:T(8,128)(2,1)}) %reduce-scatter.38.cloned.1.call-update) | async-done | bytes 329744
  675.6 81.4 %reduce-scatter.40.cloned.1.call-done = bf16[184,896]{1,0:T(8,128)(2,1)} async-done(((bf16[1472,896]{1,0:T(8,128)(2,1)}), bf16[184,896]{1,0:T(8,128)(2,1)}) %reduce-scatter.40.cloned.1.call-update) | async-done | bytes 329744
  758.8 81.7 %reduce-scatter.42.cloned.1.call-done = bf16[896,184]{0,1:T(8,128)(2,1)} async-done(((bf16[896,1472]{0,1:T(8,128)(2,1)}), bf16[896,184]{0,1:T(8,128)(2,1)}) %reduce-scatter.42.cloned.1.call-update) | async-done | bytes 329744
  842.4 8.5 rev.53
  850.9 8.4 rev.52
  864.7 8.5 rev.50
  873.2 8.5 rev.49
  957.2 40.9 %all-reduce.13 = (f32[1472]{0:T(1024)}, f32[32,6]{0,1:T(8,128)}, f32[1472]{0:T(1024)}) all-reduce(f32[1472]{0:T(1024)S(1)} %get-tuple-element.62, f32[32,6]{0,1:T(8,128)S(1)} %fusion.56, f32[1472]{0:T(1024)S(1)} %copy-done.57), channel_id=1, replica_groups=mesh['row'=8,'col'=4] {'row','col'}, use_global_device_ids=true, to_apply=%region_27.28 | all-reduce | flops 3136 | bytes 25088 | tf_op jit(solution)/shard_map/psum | solution.py:278
  1001.1 37.5 %all-reduce.17.cloned.1.call-done = (bf16[1472,96]{0,1:T(8,128)(2,1)}, bf16[1472,96]{0,1:T(8,128)(2,1)}, bf16[1472,96]{0,1:T(8,128)(2,1)}, bf16[96,1472]{1,0:T(8,128)(2,1)}) async-done(((bf16[1472,96]{0,1:T(8,128)(2,1)}, bf16[1472,96]{0,1:T(8,128)(2,1)}, bf16[1472,96]{0,1:T(8,128)(2,1)}, bf16[96,1472]{1,0:T(8,128)(2,1)}), (bf16[1472,96]{0,1:T(8,128)(2,1)}, bf16[1472,96]{0,1:T(8,128)(2,1)}, ...) | async-done | bytes 1130512
  (409 shorter events, 290.1 us)
Async XLA Ops:
  7.2 131.1 %copy-start = (f32[32,6]{0,1:T(8,128)S(1)}, f32[32,6]{0,1:T(8,128)}, u32[]{:S(2)}) copy-start(f32[32,6]{0,1:T(8,128)} %param.21) | copy-start | bytes 2308
  7.2 66.1 %copy-start.53 = (bf16[184,96]{1,0:T(8,128)(2,1)S(1)}, bf16[184,96]{1,0:T(8,128)(2,1)}, u32[]{:S(2)}) copy-start(bf16[184,96]{1,0:T(8,128)(2,1)} %param.19) | copy-start | bytes 105988
  7.2 198.7 %all-gather.12.cloned.1.call-start = ((), (), s32[]{:S(2)}) async-start(), calls=%async_computation.12 | async-start | bytes 1474560 | tf_op jit(solution)/shard_map/all_gather | solution.py:79
  41.1 176.1 %all-gather.10.cloned.1.call-start = ((), (), s32[]{:S(2)}) async-start(), calls=%async_computation.11 | async-start | bytes 1474560 | tf_op jit(solution)/shard_map/all_gather | solution.py:78
  73.3 159.5 %all-gather.14.cloned.1.call-start = ((), (), s32[]{:S(2)}) async-start(), calls=%async_computation.13 | async-start | bytes 1474560 | tf_op jit(solution)/shard_map/all_gather | solution.py:80
  105.4 142.1 %all-gather.16.cloned.1.call-start = ((), (), s32[]{:S(2)}) async-start(), calls=%async_computation.14 | async-start | bytes 1474560 | tf_op jit(solution)/shard_map/all_gather | solution.py:81
  137.3 118.6 %all-gather.20.cloned.1.call-start = ((), (), s32[]{:S(2)}) async-start(), calls=%async_computation.16 | async-start | bytes 2967552 | tf_op jit(solution)/shard_map/all_gather | solution.py:73
  137.9 142.4 %all-gather.18.cloned.1.call-start = ((), (), s32[]{:S(2)}) async-start(), calls=%async_computation.15 | async-start | bytes 3768320 | tf_op jit(solution)/shard_map/all_gather | solution.py:130
  138.2 79.1 %copy-start.67 = (f32[256]{0:T(256)}, f32[256]{0:T(256)S(1)}, u32[]{:S(2)}) copy-start(f32[256]{0:T(256)S(1)} %fusion.125) | copy-start | bytes 3076
  251.9 85.5 %all-gather.22.cloned.1.call-start = ((), (), s32[]{:S(2)}) async-start(), calls=%async_computation.17 | async-start | bytes 2967552 | tf_op jit(solution)/shard_map/all_gather | solution.py:74
  252.7 113.0 %all-gather.26.cloned.1.call-start = ((), (), s32[]{:S(2)}) async-start(), calls=%async_computation.20 | async-start | bytes 3768320 | tf_op jit(solution)/shard_map/all_gather | solution.py:138
  255.0 167.9 %all-gather.24.cloned.1.call-start = ((), (), s32[]{:S(2)}) async-start(), calls=%async_computation.18 | async-start | bytes 2967552 | tf_op jit(solution)/shard_map/all_gather | solution.py:75
  255.7 223.7 %reduce-scatter.24.cloned.1.call-start = ((), (), s32[]{:S(2)}) async-start(), calls=%async_computation.21 | async-start | bytes 3768320 | tf_op jit(solution)/shard_map/reduce_scatter | solution.py:158
  443.5 75.8 %reduce-scatter.22.cloned.1.call-start = ((), (), s32[]{:S(2)}) async-start(), calls=%async_computation.19 | async-start | bytes 3768320 | tf_op jit(solution)/shard_map/reduce_scatter | solution.py:134
  450.9 131.2 %reduce-scatter.28.cloned.1.call-start = ((), (), s32[]{:S(2)}) async-start(), calls=%async_computation.23 | async-start | bytes 983040 | tf_op jit(solution)/shard_map/reduce_scatter | solution.py:220
  540.3 49.4 %reduce-scatter.26.cloned.1.call-start = ((), (), s32[]{:S(2)}) async-start(), calls=%async_computation.22 | async-start | bytes 983040 | tf_op jit(solution)/shard_map/reduce_scatter | solution.py:217
  552.9 120.9 %reduce-scatter.38.cloned.1.call-start = ((), (), s32[]{:S(2)}) async-start(), calls=%async_computation.28 | async-start | bytes 2967552
  560.3 196.7 %reduce-scatter.40.cloned.1.call-start = ((), (), s32[]{:S(2)}) async-start(), calls=%async_computation.29 | async-start | bytes 2967552
  566.5 274.1 %reduce-scatter.42.cloned.1.call-start = ((), (), s32[]{:S(2)}) async-start(), calls=%async_computation.30 | async-start | bytes 2967552
  574.5 375.6 %reduce-scatter.36.cloned.1.call-start = ((), (), s32[]{:S(2)}) async-start(), calls=%async_computation.27 | async-start | bytes 1474560 | tf_op jit(solution)/shard_map/reduce_scatter | solution.py:251
  577.4 372.6 %reduce-scatter.30.cloned.1.call-start = ((), (), s32[]{:S(2)}) async-start(), calls=%async_computation.24 | async-start | bytes 1474560 | tf_op jit(solution)/shard_map/reduce_scatter | solution.py:242
  582.0 368.0 %reduce-scatter.34.cloned.1.call-start = ((), (), s32[]{:S(2)}) async-start(), calls=%async_computation.26 | async-start | bytes 1474560 | tf_op jit(solution)/shard_map/reduce_scatter | solution.py:248
  584.8 368.5 %reduce-scatter.32.cloned.1.call-start = ((), (), s32[]{:S(2)}) async-start(), calls=%async_computation.25 | async-start | bytes 1474560 | tf_op jit(solution)/shard_map/reduce_scatter | solution.py:245
  592.2 446.3 %all-reduce.17.cloned.1.call-start = ((), (), s32[]{:S(2)}) async-start(), calls=%async_computation.31 | async-start | bytes 2359296
  (95 other events, 534.6 us)
Sparse Core Ops, SparseCore 0:
  41.2 18.4 all-gather.11
  73.4 18.4 all-gather.9
  105.5 18.4 all-gather.13
  137.4 18.3 all-gather.15
  157.9 54.8 all-gather.19
  252.1 28.1 all-gather.17
  282.5 54.8 all-gather.21
  338.9 26.7 all-gather.25
  367.9 54.8 all-gather.23
  443.6 35.7 reduce-scatter.23
  482.1 37.1 reduce-scatter.21
  540.4 23.2 reduce-scatter.27
  566.4 23.2 reduce-scatter.25
  592.9 80.7 reduce-scatter.37
  677.1 79.8 reduce-scatter.39
  760.3 80.2 reduce-scatter.41
  843.0 25.1 reduce-scatter.35
  870.8 25.7 reduce-scatter.29
  899.2 25.7 reduce-scatter.33
  927.5 25.7 reduce-scatter.31
  957.2 81.3 all-reduce.16
where the time goes:
time: 1070 us; the launch traced here: 1050 us
  waiting for transfers between devices  507 us (47%)
  blocking collectives  185 us (17%)
  local copies, waits for them, and re-layouts  181 us (17%)
  matrix products  121 us (11%)
  other arithmetic  37.8 us (4%)
  between operations  17 us (2%)
    unnamed x25, waiting for transfers between devices  283 us
    all_gather x1, waiting for transfers between devices, body(): lax.all_gather(w_down, 'row', axis=1, tiled=True)  57.1 us
    all_gather x1, waiting for transfers between devices, body(): lax.all_gather(w_up, 'row', axis=0, tiled=True)  49.2 us
    rev x6, local copies, waits for them, and re-layouts, fold_rows(): padded = jnp.pad(matrix[::-1], ((0, 0), (0, row_total)))  44.5 us
    psum x1, blocking collectives, body(): lax.psum((grad_gain_attn_part, grad_bias_part, grad_gain_ff_part), ('row'...  40.9 us
    reduce_scatter x1, waiting for transfers between devices, body(): lax.psum_scatter(matmul(hidden_ff, full_down).astype(jnp.bfloat16), 'col'...  37 us
    all_gather x1, blocking collectives, body(): lax.all_gather(w_key, 'row', axis=0, tiled=True)  32.9 us
    dot_general x7, matrix products, matmul(): return jnp.dot(left, right, preferred_element_type=jnp.float32)  32.6 us
  transfers between devices with their start and end apart: 21, of which 12 were waited for; matrix products, arithmetic and copies ran while one was open for 25% of the time, Pallas kernels for 0%

commit v1 on v0

--- a/solution.py
+++ b/solution.py
@@ -127,7 +127,12 @@
     hidden = inputs_float + matmul(context, full_out)
     normed_ff = root_scale(hidden, gain_ff).astype(jnp.bfloat16)
     grad_out = out_grad.astype(jnp.float32) * row_mask
-    ff_rows = lax.all_gather(normed_ff, "col", axis=0, tiled=True)
+    ring = [normed_ff]
+    for hop in range(3):
+        ring.append(lax.ppermute(ring[-1], "col", [(dev, (dev + 1) % 4) for dev in range(4)]))
+    ff_rows = jnp.roll(
+        jnp.concatenate(ring[::-1], axis=0), (lax.axis_index("col") + 1) * ring[0].shape[0], axis=0
+    )
     hidden_ff = gated_product(matmul(ff_rows, full_gate), matmul(ff_rows, full_up)).astype(
         jnp.bfloat16
     )

time: 1070 us -> 998 us (0.933)
  waiting for transfers between devices: 507 us -> 432 us
  local copies, waits for them, and re-layouts: 181 us -> 192 us
    all_gather x1, waiting for transfers between devices: 57.1 us -> 0.01 us  [body(): lax.all_gather(w_down, 'row', axis=1, tiled=True)]
    all_gather x1, waiting for transfers between devices: 49.2 us -> 0.01 us  [body(): lax.all_gather(w_up, 'row', axis=0, tiled=True)]
    all_gather x1, waiting for transfers between devices: 0.02 us -> 43.9 us  [body(): lax.all_gather(w_gate, 'row', axis=0, tiled=True)]
    ppermute x0 -> x3, waiting for transfers between devices: none -> 33 us  [body(): lax.ppermute(ring[-1], 'col', [(dev, (dev + 1) % 4) for dev in range(4)])]
    all_gather x1 -> x0, waiting for transfers between devices: 24.4 us -> none  [body(): ff_rows = lax.all_gather(normed_ff, 'col', axis=0, tiled=True)]
    all_gather x1, waiting for transfers between devices: 20.4 us -> 0.01 us  [body(): lax.all_gather(grad_out.astype(jnp.bfloat16), 'col', axis=0, tiled=True)]
    unnamed x177 -> x201, local copies, waits for them, and re-layouts: 16.7 us -> 26.8 us
    unnamed x25 -> x24, waiting for transfers between devices: 283 us -> 283 us
  transfers between devices with their start and end apart: 21 -> 23, of which waited for: 12 -> 12; matrix products, arithmetic and copies ran while one was open for 25% -> 28% of each run, Pallas kernels for 0% -> 0%
where the time goes in v1:
time: 998 us; the launch traced here: 984 us
  waiting for transfers between devices  432 us (43%)
  local copies, waits for them, and re-layouts  192 us (19%)
  blocking collectives  189 us (19%)
  matrix products  118 us (12%)
  other arithmetic  34.1 us (3%)
  between operations  17 us (2%)
    unnamed x24, waiting for transfers between devices  283 us
    rev x6, local copies, waits for them, and re-layouts, fold_rows(): padded = jnp.pad(matrix[::-1], ((0, 0), (0, row_total)))  44.7 us
    all_gather x1, waiting for transfers between devices, body(): lax.all_gather(w_gate, 'row', axis=0, tiled=True)  43.9 us
    psum x1, blocking collectives, body(): lax.psum((grad_gain_attn_part, grad_bias_part, grad_gain_ff_part), ('row'...  40.8 us
    reduce_scatter x1, waiting for transfers between devices, body(): lax.psum_scatter(matmul(hidden_ff, full_down).astype(jnp.bfloat16), 'col'...  37.9 us
    dot_general x7, matrix products, matmul(): return jnp.dot(left, right, preferred_element_type=jnp.float32)  37.2 us
    ppermute x3, waiting for transfers between devices, body(): lax.ppermute(ring[-1], 'col', [(dev, (dev + 1) % 4) for dev in range(4)])  33 us
    all_gather x1, blocking collectives, body(): lax.all_gather(w_key, 'row', axis=0, tiled=True)  32.9 us
  transfers between devices with their start and end apart: 23, of which 12 were waited for; matrix products, arithmetic and copies ran while one was open for 28% of the time, Pallas kernels for 0%

profile of v1, /device:TPU:0, one launch (start us, length us, event | category | flops | bytes accessed | tf_op | source)
XLA Modules:
  0.0 983.9 jit_solution(5968595277091149170)
XLA Ops:
  7.3 32.9 %all_gather.44 = bf16[1472,96]{1,0:T(8,128)(2,1)S(1)} all-gather(bf16[184,96]{1,0:T(8,128)(2,1)} %param.18), channel_id=1, replica_groups=mesh['row'=8,'col'=4] {'row'}, dimensions={0}, use_global_device_ids=true | all-gather | bytes 317952 | tf_op jit(solution)/shard_map/all_gather | solution.py:70
  41.2 31.2 %all_gather.42 = bf16[1472,96]{1,0:T(8,128)(2,1)S(1)} all-gather(bf16[184,96]{1,0:T(8,128)(2,1)} %param.17), channel_id=1, replica_groups=mesh['row'=8,'col'=4] {'row'}, dimensions={0}, use_global_device_ids=true | all-gather | bytes 317952 | tf_op jit(solution)/shard_map/all_gather | solution.py:69
  73.3 31.1 %all_gather.47 = bf16[1472,96]{1,0:T(8,128)(2,1)S(1)} all-gather(bf16[184,96]{1,0:T(8,128)(2,1)S(1)} %copy-done.64), channel_id=1, replica_groups=mesh['row'=8,'col'=4] {'row'}, dimensions={0}, use_global_device_ids=true | all-gather | bytes 317952 | tf_op jit(solution)/shard_map/all_gather | solution.py:71
  105.4 30.9 %all_gather.50 = bf16[96,1472]{0,1:T(8,128)(2,1)S(1)} all-gather(bf16[96,184]{0,1:T(8,128)(2,1)S(1)} %copy-done.65), channel_id=1, replica_groups=mesh['row'=8,'col'=4] {'row'}, dimensions={1}, use_global_device_ids=true | all-gather | bytes 317952 | tf_op jit(solution)/shard_map/all_gather | solution.py:72
  209.9 9.1 all_gather.46
  231.1 13.4 %all_gather.49 = bf16[1024,384]{1,0:T(8,128)(2,1)S(1)} all-gather(bf16[256,384]{1,0:T(8,128)(2,1)S(1)} %convolution_convert_fusion.9), channel_id=1, replica_groups=mesh['row'=8,'col'=4] {'col'}, dimensions={0}, use_global_device_ids=true | all-gather | bytes 983040 | tf_op jit(solution)/shard_map/all_gather | solution.py:90
  251.7 10.7 %collective-permute-done = bf16[256,1472]{0,1:T(8,128)(2,1)S(1)} collective-permute-done((bf16[256,1472]{0,1:T(8,128)(2,1)S(1)}, bf16[256,1472]{0,1:T(8,128)(2,1)S(1)}, u32[]{:S(2)}, u32[]{:S(2)}) %collective-permute-start) | collective-permute-done | bytes 753696 | tf_op jit(solution)/shard_map/ppermute | solution.py:132
  263.3 11.2 %collective-permute-done.1 = bf16[256,1472]{0,1:T(8,128)(2,1)} collective-permute-done((bf16[256,1472]{0,1:T(8,128)(2,1)S(1)}, bf16[256,1472]{0,1:T(8,128)(2,1)}, u32[]{:S(2)}, u32[]{:S(2)}) %collective-permute-start.1) | collective-permute-done | bytes 753696 | tf_op jit(solution)/shard_map/ppermute | solution.py:132
  274.7 11.1 %collective-permute-done.2 = bf16[256,1472]{0,1:T(8,128)(2,1)} collective-permute-done((bf16[256,1472]{0,1:T(8,128)(2,1)}, bf16[256,1472]{0,1:T(8,128)(2,1)}, u32[]{:S(2)}, u32[]{:S(2)}) %collective-permute-start.2) | collective-permute-done | bytes 753696 | tf_op jit(solution)/shard_map/ppermute | solution.py:132
  298.6 8.0 fusion.9
  306.7 8.0 fusion.161
  314.7 43.9 %all-gather.17.cloned.1.call-done = bf16[1472,896]{1,0:T(8,128)(2,1)} async-done(((bf16[184,896]{1,0:T(8,128)(2,1)}), bf16[1472,896]{1,0:T(8,128)(2,1)}) %all-gather.17.cloned.1.call-update) | async-done | bytes 2637840 | tf_op jit(solution)/shard_map/all_gather | solution.py:73
  358.5 12.7 %multiply_convert_fusion = (bf16[1024,896]{1,0:T(8,128)(2,1)S(1)}, bf16[1024,896]{1,0:T(8,128)(2,1)S(1)}, bf16[1024,896]{1,0:T(8,128)(2,1)}) fusion(f32[1024,896]{1,0:T(8,128)} %fusion.161, f32[1024,896]{1,0:T(8,128)} %fusion.9, bf16[1472,896]{1,0:T(8,128)(2,1)} %all-gather.17.cloned.1.call-done, bf16[2048,1472]{0,1:T(8,128)(2,1)} %constant_dynamic-update-slice_fusion, ...), kind=kOutput, calls=%fused_computation.11 | convolution fusion | flops 2724986880 | bytes 18497540 | tf_op jit(solution)/shard_map/dot_general | solution.py:29
  387.2 28.0 %reduce-scatter.24.cloned.1.call-done = bf16[256,1472]{0,1:T(8,128)(2,1)} async-done(((bf16[1024,1472]{0,1:T(8,128)(2,1)}), bf16[256,1472]{0,1:T(8,128)(2,1)}) %reduce-scatter.24.cloned.1.call-update) | async-done | bytes 753680 | tf_op jit(solution)/shard_map/reduce_scatter | solution.py:163
  417.2 37.9 %reduce-scatter.22.cloned.1.call-done = bf16[256,1472]{0,1:T(8,128)(2,1)} async-done(((bf16[1024,1472]{0,1:T(8,128)(2,1)}), bf16[256,1472]{0,1:T(8,128)(2,1)}) %reduce-scatter.22.cloned.1.call-update) | async-done | bytes 753680 | tf_op jit(solution)/shard_map/reduce_scatter | solution.py:139
  525.4 80.6 %reduce-scatter.40.cloned.1.call-done = bf16[184,896]{1,0:T(8,128)(2,1)} async-done(((bf16[1472,896]{1,0:T(8,128)(2,1)}), bf16[184,896]{1,0:T(8,128)(2,1)}) %reduce-scatter.40.cloned.1.call-update) | async-done | bytes 329744
  607.8 82.0 %reduce-scatter.38.cloned.1.call-done = bf16[184,896]{1,0:T(8,128)(2,1)} async-done(((bf16[1472,896]{1,0:T(8,128)(2,1)}), bf16[184,896]{1,0:T(8,128)(2,1)}) %reduce-scatter.38.cloned.1.call-update) | async-done | bytes 329744
  691.7 81.4 %reduce-scatter.42.cloned.1.call-done = bf16[896,184]{0,1:T(8,128)(2,1)} async-done(((bf16[896,1472]{0,1:T(8,128)(2,1)}), bf16[896,184]{0,1:T(8,128)(2,1)}) %reduce-scatter.42.cloned.1.call-update) | async-done | bytes 329744
  775.0 8.6 rev.53
  783.7 8.4 rev.52
  797.5 8.5 rev.50
  806.0 8.5 rev.49
  889.7 40.8 %all-reduce.13 = (f32[1472]{0:T(1024)}, f32[32,6]{0,1:T(8,128)}, f32[1472]{0:T(1024)}) all-reduce(f32[1472]{0:T(1024)S(1)} %get-tuple-element.62, f32[32,6]{0,1:T(8,128)S(1)} %fusion.62, f32[1472]{0:T(1024)S(1)} %get-tuple-element.60), channel_id=1, replica_groups=mesh['row'=8,'col'=4] {'row','col'}, use_global_device_ids=true, to_apply=%region_27.28 | all-reduce | flops 3136 | bytes 25088 | tf_op jit(solution)/shard_map/psum | solution.py:283
  933.5 37.5 %all-reduce.17.cloned.1.call-done = (bf16[1472,96]{0,1:T(8,128)(2,1)}, bf16[1472,96]{0,1:T(8,128)(2,1)}, bf16[1472,96]{0,1:T(8,128)(2,1)}, bf16[96,1472]{1,0:T(8,128)(2,1)}) async-done(((bf16[1472,96]{0,1:T(8,128)(2,1)}, bf16[1472,96]{0,1:T(8,128)(2,1)}, bf16[1472,96]{0,1:T(8,128)(2,1)}, bf16[96,1472]{1,0:T(8,128)(2,1)}), (bf16[1472,96]{0,1:T(8,128)(2,1)}, bf16[1472,96]{0,1:T(8,128)(2,1)}, ...) | async-done | bytes 1130512
  (438 shorter events, 290.3 us)
Async XLA Ops:
  7.2 133.6 %copy-start = (f32[32,6]{0,1:T(8,128)S(1)}, f32[32,6]{0,1:T(8,128)}, u32[]{:S(2)}) copy-start(f32[32,6]{0,1:T(8,128)} %param.21) | copy-start | bytes 2308
  7.2 200.5 %all-gather.11.cloned.1.call-start = ((), (), s32[]{:S(2)}) async-start(), calls=%async_computation.12 | async-start | bytes 1474560 | tf_op jit(solution)/shard_map/all_gather | solution.py:79
  41.1 177.9 %all-gather.9.cloned.1.call-start = ((), (), s32[]{:S(2)}) async-start(), calls=%async_computation.11 | async-start | bytes 1474560 | tf_op jit(solution)/shard_map/all_gather | solution.py:78
  73.3 155.3 %all-gather.13.cloned.1.call-start = ((), (), s32[]{:S(2)}) async-start(), calls=%async_computation.13 | async-start | bytes 1474560 | tf_op jit(solution)/shard_map/all_gather | solution.py:80
  105.4 142.9 %all-gather.15.cloned.1.call-start = ((), (), s32[]{:S(2)}) async-start(), calls=%async_computation.14 | async-start | bytes 1474560 | tf_op jit(solution)/shard_map/all_gather | solution.py:81
  137.3 161.3 %all-gather.19.cloned.1.call-start = ((), (), s32[]{:S(2)}) async-start(), calls=%async_computation.16 | async-start | bytes 2967552 | tf_op jit(solution)/shard_map/all_gather | solution.py:74
  137.9 168.8 %all-gather.23.cloned.1.call-start = ((), (), s32[]{:S(2)}) async-start(), calls=%async_computation.19 | async-start | bytes 3768320 | tf_op jit(solution)/shard_map/all_gather | solution.py:143
  139.7 167.0 %all-gather.21.cloned.1.call-start = ((), (), s32[]{:S(2)}) async-start(), calls=%async_computation.17 | async-start | bytes 2967552 | tf_op jit(solution)/shard_map/all_gather | solution.py:75
  140.4 218.1 %all-gather.17.cloned.1.call-start = ((), (), s32[]{:S(2)}) async-start(), calls=%async_computation.15 | async-start | bytes 2967552 | tf_op jit(solution)/shard_map/all_gather | solution.py:73
  251.3 11.1 %collective-permute-start = (bf16[256,1472]{0,1:T(8,128)(2,1)S(1)}, bf16[256,1472]{0,1:T(8,128)(2,1)S(1)}, u32[]{:S(2)}, u32[]{:S(2)}) collective-permute-start(bf16[256,1472]{0,1:T(8,128)(2,1)S(1)} %multiply_convert_fusion.3), channel_id=1, source_target_pairs={{0,1},{1,2},{2,3},{3,0},{4,5},{5,6},{6,7},{7,4},{8,9},{9,10},{10,1... | collective-permute-start | bytes 2261000 | tf_op jit(solution)/shard_map/ppermute | solution.py:132
  263.3 11.2 %collective-permute-start.1 = (bf16[256,1472]{0,1:T(8,128)(2,1)S(1)}, bf16[256,1472]{0,1:T(8,128)(2,1)}, u32[]{:S(2)}, u32[]{:S(2)}) collective-permute-start(bf16[256,1472]{0,1:T(8,128)(2,1)S(1)} %collective-permute-done), channel_id=1, source_target_pairs={{0,1},{1,2},{2,3},{3,0},{4,5},{5,6},{6,7},{7,4},{8,9},{9,10},{10,1... | collective-permute-start | bytes 2261000 | tf_op jit(solution)/shard_map/ppermute | solution.py:132
  274.4 11.4 %collective-permute-start.2 = (bf16[256,1472]{0,1:T(8,128)(2,1)}, bf16[256,1472]{0,1:T(8,128)(2,1)}, u32[]{:S(2)}, u32[]{:S(2)}) collective-permute-start(bf16[256,1472]{0,1:T(8,128)(2,1)} %collective-permute-done.1), channel_id=1, source_target_pairs={{0,1},{1,2},{2,3},{3,0},{4,5},{5,6},{6,7},{7,4},{8,9},{9,10},{10,1... | collective-permute-start | bytes 2261000 | tf_op jit(solution)/shard_map/ppermute | solution.py:132
  274.5 140.8 %reduce-scatter.24.cloned.1.call-start = ((), (), s32[]{:S(2)}) async-start(), calls=%async_computation.20 | async-start | bytes 3768320 | tf_op jit(solution)/shard_map/reduce_scatter | solution.py:163
  379.4 75.6 %reduce-scatter.22.cloned.1.call-start = ((), (), s32[]{:S(2)}) async-start(), calls=%async_computation.18 | async-start | bytes 3768320 | tf_op jit(solution)/shard_map/reduce_scatter | solution.py:139
  386.8 129.2 %reduce-scatter.28.cloned.1.call-start = ((), (), s32[]{:S(2)}) async-start(), calls=%async_computation.22 | async-start | bytes 983040 | tf_op jit(solution)/shard_map/reduce_scatter | solution.py:225
  472.3 49.3 %reduce-scatter.26.cloned.1.call-start = ((), (), s32[]{:S(2)}) async-start(), calls=%async_computation.21 | async-start | bytes 983040 | tf_op jit(solution)/shard_map/reduce_scatter | solution.py:222
  484.4 121.6 %reduce-scatter.40.cloned.1.call-start = ((), (), s32[]{:S(2)}) async-start(), calls=%async_computation.28 | async-start | bytes 2967552
  491.8 198.1 %reduce-scatter.38.cloned.1.call-start = ((), (), s32[]{:S(2)}) async-start(), calls=%async_computation.27 | async-start | bytes 2967552
  499.7 273.5 %reduce-scatter.42.cloned.1.call-start = ((), (), s32[]{:S(2)}) async-start(), calls=%async_computation.29 | async-start | bytes 2967552
  507.6 375.0 %reduce-scatter.36.cloned.1.call-start = ((), (), s32[]{:S(2)}) async-start(), calls=%async_computation.26 | async-start | bytes 1474560 | tf_op jit(solution)/shard_map/reduce_scatter | solution.py:256
  510.6 372.1 %reduce-scatter.30.cloned.1.call-start = ((), (), s32[]{:S(2)}) async-start(), calls=%async_computation.23 | async-start | bytes 1474560 | tf_op jit(solution)/shard_map/reduce_scatter | solution.py:247
  515.9 366.8 %reduce-scatter.34.cloned.1.call-start = ((), (), s32[]{:S(2)}) async-start(), calls=%async_computation.25 | async-start | bytes 1474560 | tf_op jit(solution)/shard_map/reduce_scatter | solution.py:253
  518.6 367.2 %reduce-scatter.32.cloned.1.call-start = ((), (), s32[]{:S(2)}) async-start(), calls=%async_computation.24 | async-start | bytes 1474560 | tf_op jit(solution)/shard_map/reduce_scatter | solution.py:250
  524.1 446.8 %all-reduce.17.cloned.1.call-start = ((), (), s32[]{:S(2)}) async-start(), calls=%async_computation.30 | async-start | bytes 2359296
  (106 other events, 900.1 us)
Sparse Core Ops, SparseCore 0:
  41.2 18.4 all-gather.10
  73.4 18.4 all-gather.8
  105.5 18.4 all-gather.12
  137.4 18.3 all-gather.14
  157.9 54.8 all-gather.18
  214.8 30.9 all-gather.22
  248.0 54.8 all-gather.20
  305.1 53.4 all-gather.16
  379.5 35.6 reduce-scatter.23
  417.8 37.1 reduce-scatter.21
  472.4 23.2 reduce-scatter.27
  498.3 23.2 reduce-scatter.25
  525.0 80.9 reduce-scatter.39
  609.3 80.5 reduce-scatter.37
  693.1 79.9 reduce-scatter.41
  775.6 25.1 reduce-scatter.35
  803.4 25.6 reduce-scatter.29
  831.6 25.7 reduce-scatter.33
  860.1 25.7 reduce-scatter.31
  889.5 81.3 all-reduce.16
